TPU v7x, 32 devices: a whole 2x2x4 slice. The times are simulated.
32 devices in a mesh: seg: 4 (over z), pair: 8 (over y, x, core).
Axes of the slice: x: 2, y: 2, z: 4, core: 2. Of those that a mesh axis runs over, the one named last changes fastest.
Arguments:
- spectra: bfloat16 [4, 2, 2048, 2048], P('seg', None, None, 'pair'), may hold values from -6 to 6
- pair_lists: int32 [32, 2], P('pair'), may hold values from 0 to 15
- pair_counts: int32 [8], P('pair'), may hold values from 1 to 4, as said below
Outputs:
- correlations: float32 [2048, 32, 128], P('seg', 'pair')
Inputs may be any that keep to these rules, and one draw needn't show every extreme that they name: `pair_counts`: some owner uses exactly 4 slots.
All inputs are finite; a program needn't handle non-finite values.
Results may differ from a plain program's by a relative error of at most 0.0003.
Values may be sent and summed in bfloat16 or wider, within the bound.
No kernel may reach another device: no remote copies, remote signals or barrier semaphores. Data moves between devices by JAX's collectives and lax.ppermute only.
A program may use at most 128 MiB of HBM per device.

v0:
```python
import math
import jax
import jax.numpy as jnp
from jax import lax
from jax.sharding import PartitionSpec as P

TILE = 128
LAG = 2048


def stack_weights(linear_re, linear_im, phase_re, phase_im, total_segments):
    weight = (phase_re * phase_re + phase_im * phase_im) / float(total_segments * total_segments)
    return (linear_re * weight, linear_im * weight)


def accumulate(local_spec, group, source_ids, receiver_ids):
    segs_here = local_spec.shape[0]
    band_bins = local_spec.shape[2]
    tiled_spec = local_spec.reshape(segs_here // group, group, 2, band_bins, -1, TILE)

    def one_group(totals, block):
        source_spec = jnp.take(block, source_ids, axis=3).astype(jnp.float32)
        recv_spec = jnp.take(block, receiver_ids, axis=3).astype(jnp.float32)
        cross_re = source_spec[:, 0] * recv_spec[:, 0] + source_spec[:, 1] * recv_spec[:, 1]
        cross_im = source_spec[:, 1] * recv_spec[:, 0] - source_spec[:, 0] * recv_spec[:, 1]
        magnitude = jnp.sqrt(cross_re * cross_re + cross_im * cross_im + 1.0)
        return (
            (
                totals[0] + jnp.sum(cross_re, axis=0),
                totals[1] + jnp.sum(cross_im, axis=0),
                totals[2] + jnp.sum(cross_re / magnitude, axis=0),
                totals[3] + jnp.sum(cross_im / magnitude, axis=0),
            ),
            None,
        )

    zeros = jnp.zeros((band_bins, source_ids.shape[0], TILE), jnp.float32)
    sums, _ = lax.scan(one_group, (zeros, zeros, zeros, zeros), tiled_spec)
    return sums


def body(spectra, pair_lists, pair_counts):
    seg_dev = spectra.shape[0]
    freq_bins = spectra.shape[2]
    n_pair = lax.axis_size("pair")
    n_seg = lax.axis_size("seg")
    seg_index = lax.axis_index("seg")
    most_slots = pair_lists.shape[0]
    total_segments = seg_dev * n_seg
    lists = lax.all_gather(pair_lists, "pair", axis=0, tiled=True)
    source_ids = lists[:, 0]
    receiver_ids = lists[:, 1]
    sub_bins = freq_bins // (n_pair * n_seg)
    bands = lax.all_to_all(spectra, "pair", split_axis=2, concat_axis=3, tiled=True)
    partial_sums = accumulate(bands, seg_dev, source_ids, receiver_ids)
    shares = (
        lax.psum_scatter(partial_sums[0], "seg", scatter_dimension=0, tiled=True),
        lax.psum_scatter(partial_sums[1], "seg", scatter_dimension=0, tiled=True),
        lax.psum_scatter(partial_sums[2], "seg", scatter_dimension=0, tiled=True),
        lax.psum_scatter(partial_sums[3], "seg", scatter_dimension=0, tiled=True),
    )
    block_start = jnp.arange(n_pair, dtype=jnp.int32) * (freq_bins // n_pair) + seg_index * sub_bins
    stack_re, stack_im = stack_weights(shares[0], shares[1], shares[2], shares[3], total_segments)
    stack_re = stack_re.reshape(sub_bins, n_pair, most_slots, TILE)
    stack_im = stack_im.reshape(sub_bins, n_pair, most_slots, TILE)
    owned = (
        lax.all_to_all(stack_re, "pair", split_axis=1, concat_axis=0, tiled=True),
        lax.all_to_all(stack_im, "pair", split_axis=1, concat_axis=0, tiled=True),
    )
    own_bins = sub_bins * n_pair
    row_index = jnp.arange(own_bins, dtype=jnp.int32)
    bin_index = block_start[row_index // sub_bins] + row_index % sub_bins
    owned_re = owned[0].reshape(own_bins, most_slots, TILE)
    owned_im = owned[1].reshape(own_bins, most_slots, TILE)
    live_mask = (jnp.arange(most_slots, dtype=jnp.int32) < pair_counts[0]).astype(jnp.float32)
    owned_re = (owned_re * live_mask[None, :, None]).reshape(own_bins, most_slots * TILE)
    owned_im = (owned_im * live_mask[None, :, None]).reshape(own_bins, most_slots * TILE)
    lag_rows = LAG // n_seg
    lag_offset = jnp.arange(lax.axis_size("seg") * lag_rows, dtype=jnp.int32) - LAG // 2
    product = lag_offset[:, None] * bin_index[None, :] % (2 * freq_bins)
    angles = product.astype(jnp.float32) * jnp.float32(math.pi / freq_bins)
    terms = jnp.dot(
        jnp.cos(angles),
        owned_re,
        precision=lax.Precision.HIGHEST,
        preferred_element_type=jnp.float32,
    )
    terms = terms - jnp.dot(
        jnp.sin(angles),
        owned_im,
        precision=lax.Precision.HIGHEST,
        preferred_element_type=jnp.float32,
    )
    summed = lax.psum_scatter(
        terms * jnp.float32(1.0 / math.sqrt(freq_bins)), "seg", scatter_dimension=0, tiled=True
    )
    return summed.reshape(lag_rows, most_slots, TILE)


def solution(mesh):
    return jax.shard_map(
        body,
        mesh=mesh,
        in_specs=(P("seg", None, None, "pair"), P("pair", None), P("pair")),
        out_specs=P("seg", "pair", None),
        check_vma=False,
    )
```

profile of v0, /device:TPU:0, one launch (start us, length us, event | category | flops | bytes accessed | tf_op | source)
XLA Modules:
  0.0 561.9 jit_solution(8158701286742860428)
XLA Ops:
  6.5 5.8 %copy.27 = bf16[1,2,2048,256]{3,1,0,2:T(2,128)(2,1)} copy(bf16[1,2,2048,256]{3,2,1,0:T(8,128)(2,1)} %param.5) | data formatting | bytes 4194304 | tf_op args[0]
  12.3 5.2 all-to-all-start
  17.6 29.6 %all-gather = s32[8,4,2]{1,2,0:T(2,128)S(1)} all-gather(s32[1,4,2]{1,2,0:T(2,128)S(1)} %bitcast.100), channel_id=1, replica_groups=mesh['seg'=4,'pair'=8] {'pair'}, dimensions={0}, use_global_device_ids=true | all-gather | bytes 288 | tf_op jit(solution)/shard_map/all_gather | solution.py:50
  47.3 1.6 copy.28
  48.9 4.0 copy.29
  52.9 3.0 copy.30
  55.9 3.1 gather_fusion
  59.0 3.0 gather_fusion.1
  62.0 2.9 fusion.4
  65.4 0.7 fusion.3
  66.1 6.3 %fusion.11 = (f32[256,32,128]{2,0,1:T(8,128)}, f32[256,32,128]{2,0,1:T(8,128)}, f32[256,32,128]{2,0,1:T(8,128)}) fusion(f32[1,2,256,32,128]{4,2,3,1,0:T(8,128)S(1)} %fusion.3, f32[1,2,256,32,128]{4,2,1,3,0:T(8,128)S(1)} %fusion.4), kind=kLoop, calls=%fused_computation.26 | loop fusion | flops 11534336 | bytes 29360128 | tf_op jit(solution)/shard_map/while/body/eval_jaxpr/div | solution.py:31
  72.4 6.4 %fusion.10 = f32[256,32,128]{2,0,1:T(8,128)} fusion(f32[256,32,128]{2,0,1:T(8,128)} %get-tuple-element.22, f32[256,32,128]{2,0,1:T(8,128)} %get-tuple-element.21), kind=kLoop, calls=%fused_computation.25 | loop fusion | flops 5242880 | bytes 12582912 | tf_op jit(solution)/shard_map/while/body/eval_jaxpr/div | solution.py:32
  78.9 0.7 reduce-scatter.12.cloned.1.call-update
  79.7 0.7 reduce-scatter.6.cloned.1.call-update
  80.4 0.5 reduce-scatter.8.cloned.1.call-update
  81.0 74.2 %reduce-scatter.10.cloned.1.call-done = f32[64,32,128]{2,0,1:T(8,128)} async-done(((f32[256,32,128]{2,0,1:T(8,128)}), f32[64,32,128]{2,0,1:T(8,128)}) %reduce-scatter.10.cloned.1.call-update) | async-done | bytes 1048592 | tf_op jit(solution)/shard_map/reduce_scatter | solution.py:60
  155.2 79.7 %reduce-scatter.12.cloned.1.call-done = f32[64,32,128]{2,0,1:T(8,128)} async-done(((f32[256,32,128]{2,0,1:T(8,128)}), f32[64,32,128]{2,0,1:T(8,128)}) %reduce-scatter.12.cloned.1.call-update) | async-done | bytes 1048592 | tf_op jit(solution)/shard_map/reduce_scatter | solution.py:58
  234.9 79.6 %reduce-scatter.6.cloned.1.call-done = f32[64,32,128]{2,0,1:T(8,128)} async-done(((f32[256,32,128]{2,0,1:T(8,128)}), f32[64,32,128]{2,0,1:T(8,128)}) %reduce-scatter.6.cloned.1.call-update) | async-done | bytes 1048592 | tf_op jit(solution)/shard_map/reduce_scatter | solution.py:57
  314.5 79.6 %reduce-scatter.8.cloned.1.call-done = f32[64,32,128]{2,0,1:T(8,128)} async-done(((f32[256,32,128]{2,0,1:T(8,128)}), f32[64,32,128]{2,0,1:T(8,128)}) %reduce-scatter.8.cloned.1.call-update) | async-done | bytes 1048592 | tf_op jit(solution)/shard_map/reduce_scatter | solution.py:59
  394.1 2.6 fusion.23
  396.7 1.6 copy.38
  398.3 3.6 all-to-all-start.2
  402.7 0.7 fusion.38
  403.4 1.6 copy.37
  405.0 12.4 %all-to-all-done.2 = f32[64,8,4,128]{3,2,0,1:T(4,128)S(1)} async-done(((f32[64,8,4,128]{3,2,0,1:T(4,128)}), f32[64,8,4,128]{3,2,0,1:T(4,128)S(1)}, u32[]{:S(2)}, u32[]{:S(2)}) %all-to-all-start.2) | async-done | bytes 1048608 | tf_op jit(solution)/shard_map/all_to_all | solution.py:68
  417.4 3.6 all-to-all-start.1
  421.2 4.3 compare_select_fusion.1
  425.5 0.6 fusion.24
  426.1 23.5 %fusion.8 = f32[2048,512]{1,0:T(8,128)} fusion(s32[512]{0:T(512)S(1)} %fusion.24, s32[2048]{0:T(1024)S(1)} %iota_add_fusion, f32[64,8,4,128]{3,2,1,0:T(4,128)S(1)} %bitcast.97, f32[512]{0:T(512)S(1)} %broadcast_bitcast_fusion), kind=kOutput, calls=%fused_computation.22 | convolution fusion | flops 6457393152 | bytes 5255168 | tf_op jit(solution)/shard_map/dot_general | solution.py:88
  449.6 25.5 %subtract_multiply_fusion = f32[2048,512]{1,0:T(8,128)} fusion(f32[2048,512]{1,0:T(8,128)} %fusion.8, s32[512]{0:T(512)S(1)} %fusion.24, s32[2048]{0:T(1024)S(1)} %iota_add_fusion, f32[64,8,4,128]{3,2,1,0:T(4,128)S(1)} %bitcast.98, f32[512]{0:T(512)S(1)} %broadcast_bitcast_fusion), kind=kOutput, calls=%fused_computation.21 | convolution fusion | flops 6459490304 | bytes 9449472 | tf_op jit(solution)/shard_map/dot_general | solution.py:82
  475.2 77.7 %reduce-scatter.14.cloned.1.call-done = f32[512,512]{1,0:T(8,128)} async-done(((f32[2048,512]{1,0:T(8,128)}), f32[512,512]{1,0:T(8,128)}) %reduce-scatter.14.cloned.1.call-update) | async-done | bytes 1048592 | tf_op jit(solution)/shard_map/reduce_scatter | solution.py:94
  552.8 2.5 reshape.186
  (22 shorter events, 1.1 us)
Async XLA Ops:
  6.5 11.0 %copy-start.1 = (s32[4,2]{0,1:T(2,128)S(1)}, s32[4,2]{0,1:T(2,128)}, u32[]{:S(2)}) copy-start(s32[4,2]{0,1:T(2,128)} %param.6) | copy-start | bytes 100
  12.3 35.0 %all-to-all-start = ((bf16[1,2,2048,256]{3,1,0,2:T(2,128)(2,1)}), bf16[1,2,2048,256]{3,1,0,2:T(2,128)(2,1)S(1)}, u32[]{:S(2)}, u32[]{:S(2)}) async-start(bf16[1,2,2048,256]{3,1,0,2:T(2,128)(2,1)} %copy.27), calls=%async_computation | async-start | bytes 4194304 | tf_op jit(solution)/shard_map/all_to_all | solution.py:54
  17.5 137.7 %reduce-scatter.10.cloned.1.call-start = ((), (), s32[]{:S(2)}) async-start(), calls=%async_computation.10 | async-start | bytes 5242880 | tf_op jit(solution)/shard_map/reduce_scatter | solution.py:60
  62.0 3.4 copy-start
  78.9 156.0 %reduce-scatter.12.cloned.1.call-start = ((), (), s32[]{:S(2)}) async-start(), calls=%async_computation.11 | async-start | bytes 5242880 | tf_op jit(solution)/shard_map/reduce_scatter | solution.py:58
  79.6 234.8 %reduce-scatter.6.cloned.1.call-start = ((), (), s32[]{:S(2)}) async-start(), calls=%async_computation.8 | async-start | bytes 5242880 | tf_op jit(solution)/shard_map/reduce_scatter | solution.py:57
  80.4 313.7 %reduce-scatter.8.cloned.1.call-start = ((), (), s32[]{:S(2)}) async-start(), calls=%async_computation.9 | async-start | bytes 5242880 | tf_op jit(solution)/shard_map/reduce_scatter | solution.py:59
  398.3 19.1 %all-to-all-start.2 = ((f32[64,8,4,128]{3,2,0,1:T(4,128)}), f32[64,8,4,128]{3,2,0,1:T(4,128)S(1)}, u32[]{:S(2)}, u32[]{:S(2)}) async-start(f32[64,8,4,128]{3,2,0,1:T(4,128)} %copy.38), calls=%async_computation.6 | async-start | bytes 2097152 | tf_op jit(solution)/shard_map/all_to_all | solution.py:68
  417.4 32.3 %all-to-all-start.1 = ((f32[64,8,4,128]{3,2,0,1:T(4,128)}), f32[64,8,4,128]{3,2,0,1:T(4,128)S(1)}, u32[]{:S(2)}, u32[]{:S(2)}) async-start(f32[64,8,4,128]{3,2,0,1:T(4,128)} %copy.37), calls=%async_computation.4 | async-start | bytes 2097152 | tf_op jit(solution)/shard_map/all_to_all | solution.py:67
  420.9 131.9 %reduce-scatter.14.cloned.1.call-start = ((), (), s32[]{:S(2)}) async-start(), calls=%async_computation.12 | async-start | bytes 5242880 | tf_op jit(solution)/shard_map/reduce_scatter | solution.py:94
Sparse Core Ops, SparseCore 0:
  79.0 76.1 reduce-scatter.9
  157.6 77.2 reduce-scatter.11
  237.2 77.2 reduce-scatter.5
  316.7 77.2 reduce-scatter.7
  475.3 77.5 reduce-scatter.13
where the time goes:
time: 563 us; the launch traced here: 562 us
  waiting for transfers between devices  405 us (72%)
  matrix products  49 us (9%)
  blocking collectives  29.6 us (5%)
  local copies, waits for them, and re-layouts  27.6 us (5%)
  other arithmetic  23.9 us (4%)
  between operations  13.9 us (2%)
  starting transfers between devices  12.7 us (2%)
    reduce_scatter x1, waiting for transfers between devices, body(): lax.psum_scatter(partial_sums[1], 'seg', scatter_dimension=0, tiled=True)  79.7 us
    reduce_scatter x1, waiting for transfers between devices, body(): lax.psum_scatter(partial_sums[0], 'seg', scatter_dimension=0, tiled=True)  79.6 us
    reduce_scatter x1, waiting for transfers between devices, body(): lax.psum_scatter(partial_sums[2], 'seg', scatter_dimension=0, tiled=True)  79.6 us
    reduce_scatter x1, waiting for transfers between devices, body(): lax.psum_scatter(terms * jnp.float32(1.0 / math.sqrt(freq_bins)), 'seg',...  77.7 us
    reduce_scatter x1, waiting for transfers between devices, body(): lax.psum_scatter(partial_sums[3], 'seg', scatter_dimension=0, tiled=True)  74.2 us
    all_gather x1, blocking collectives, body(): lists = lax.all_gather(pair_lists, 'pair', axis=0, tiled=True)  29.6 us
    dot_general x1, matrix products, body(): jnp.dot(jnp.cos(angles), owned_re, precision=lax.Precision.HIGHEST, prefe...  25.5 us
    dot_general x1, matrix products, body(): jnp.dot(jnp.sin(angles), owned_im, precision=lax.Precision.HIGHEST, prefe...  23.5 us
  transfers between devices with their start and end apart: 8, of which 6 were waited for; matrix products, arithmetic and copies ran while one was open for 6% of the time, Pallas kernels for 0%

commit v1 on v0

--- a/solution.py
+++ b/solution.py
@@ -47,7 +47,12 @@
     seg_index = lax.axis_index("seg")
     most_slots = pair_lists.shape[0]
     total_segments = seg_dev * n_seg
-    lists = lax.all_gather(pair_lists, "pair", axis=0, tiled=True)
+    ring = [pair_lists]
+    for hop in range(7):
+        ring.append(lax.ppermute(ring[-1], "pair", [(dev, (dev + 1) % 8) for dev in range(8)]))
+    lists = jnp.roll(
+        jnp.concatenate(ring[::-1], axis=0), (lax.axis_index("pair") + 1) * ring[0].shape[0], axis=0
+    )
     source_ids = lists[:, 0]
     receiver_ids = lists[:, 1]
     sub_bins = freq_bins // (n_pair * n_seg)

time: 563 us -> 583 us (1.036)
  waiting for transfers between devices: 405 us -> 454 us
  blocking collectives: 29.6 us -> 0 us
    ppermute x0 -> x7, waiting for transfers between devices: none -> 49 us  [body(): lax.ppermute(ring[-1], 'pair', [(dev, (dev + 1) % 8) for dev in range(8)])]
    all_gather x1 -> x0, blocking collectives: 29.6 us -> none  [body(): lists = lax.all_gather(pair_lists, 'pair', axis=0, tiled=True)]
  transfers between devices with their start and end apart: 8 -> 15, of which waited for: 6 -> 13; matrix products, arithmetic and copies ran while one was open for 6% -> 5% of each run, Pallas kernels for 0% -> 0%
where the time goes in v1:
time: 583 us; the launch traced here: 582 us
  waiting for transfers between devices  454 us (78%)
  matrix products  49.1 us (8%)
  local copies, waits for them, and re-layouts  27.8 us (5%)
  other arithmetic  24 us (4%)
  between operations  13.9 us (2%)
  starting transfers between devices  13.3 us (2%)
    reduce_scatter x1, waiting for transfers between devices, body(): lax.psum_scatter(partial_sums[1], 'seg', scatter_dimension=0, tiled=True)  79.7 us
    reduce_scatter x1, waiting for transfers between devices, body(): lax.psum_scatter(partial_sums[0], 'seg', scatter_dimension=0, tiled=True)  79.6 us
    reduce_scatter x1, waiting for transfers between devices, body(): lax.psum_scatter(partial_sums[2], 'seg', scatter_dimension=0, tiled=True)  79.5 us
    reduce_scatter x1, waiting for transfers between devices, body(): lax.psum_scatter(terms * jnp.float32(1.0 / math.sqrt(freq_bins)), 'seg',...  77.7 us
    reduce_scatter x1, waiting for transfers between devices, body(): lax.psum_scatter(partial_sums[3], 'seg', scatter_dimension=0, tiled=True)  74.2 us
    ppermute x7, waiting for transfers between devices, body(): lax.ppermute(ring[-1], 'pair', [(dev, (dev + 1) % 8) for dev in range(8)])  49 us
    dot_general x1, matrix products, body(): jnp.dot(jnp.cos(angles), owned_re, precision=lax.Precision.HIGHEST, prefe...  25.5 us
    dot_general x1, matrix products, body(): jnp.dot(jnp.sin(angles), owned_im, precision=lax.Precision.HIGHEST, prefe...  23.5 us
  transfers between devices with their start and end apart: 15, of which 13 were waited for; matrix products, arithmetic and copies ran while one was open for 5% of the time, Pallas kernels for 0%

profile of v1, /device:TPU:0, one launch (start us, length us, event | category | flops | bytes accessed | tf_op | source)
XLA Modules:
  0.0 582.1 jit_solution(2251575107313372012)
XLA Ops:
  6.5 5.8 copy.23
  12.3 5.2 all-to-all-start
  18.1 25.7 %collective-permute-done = s32[4,2]{0,1:T(2,128)S(1)} collective-permute-done((s32[4,2]{0,1:T(2,128)S(1)}, s32[4,2]{0,1:T(2,128)S(1)}, u32[]{:S(2)}, u32[]{:S(2)}) %collective-permute-start) | collective-permute-done | bytes 64 | tf_op jit(solution)/shard_map/ppermute | solution.py:52
  43.7 3.9 collective-permute-done.1
  47.6 3.9 collective-permute-done.2
  51.5 3.9 collective-permute-done.3
  55.4 3.9 collective-permute-done.4
  59.3 3.9 collective-permute-done.5
  63.2 3.9 collective-permute-done.6
  67.3 1.6 copy.24
  69.0 4.0 copy.25
  72.9 3.0 copy.26
  75.9 3.1 gather_fusion
  79.0 3.0 gather_fusion.1
  82.1 2.9 fusion.4
  86.2 6.3 %fusion.11 = (f32[256,32,128]{2,0,1:T(8,128)}, f32[256,32,128]{2,0,1:T(8,128)}, f32[256,32,128]{2,0,1:T(8,128)}) fusion(f32[1,2,256,32,128]{4,2,3,1,0:T(8,128)S(1)} %fusion.3, f32[1,2,256,32,128]{4,2,1,3,0:T(8,128)S(1)} %fusion.4), kind=kLoop, calls=%fused_computation.26 | loop fusion | flops 11534336 | bytes 29360128 | tf_op jit(solution)/shard_map/while/body/eval_jaxpr/div | solution.py:31
  92.5 6.4 %fusion.10 = f32[256,32,128]{2,0,1:T(8,128)} fusion(f32[256,32,128]{2,0,1:T(8,128)} %get-tuple-element.22, f32[256,32,128]{2,0,1:T(8,128)} %get-tuple-element.21), kind=kLoop, calls=%fused_computation.25 | loop fusion | flops 5242880 | bytes 12582912 | tf_op jit(solution)/shard_map/while/body/eval_jaxpr/div | solution.py:32
  101.0 74.2 %reduce-scatter.10.cloned.1.call-done = f32[64,32,128]{2,0,1:T(8,128)} async-done(((f32[256,32,128]{2,0,1:T(8,128)}), f32[64,32,128]{2,0,1:T(8,128)}) %reduce-scatter.10.cloned.1.call-update) | async-done | bytes 1048592 | tf_op jit(solution)/shard_map/reduce_scatter | solution.py:65
  175.3 79.7 %reduce-scatter.12.cloned.1.call-done = f32[64,32,128]{2,0,1:T(8,128)} async-done(((f32[256,32,128]{2,0,1:T(8,128)}), f32[64,32,128]{2,0,1:T(8,128)}) %reduce-scatter.12.cloned.1.call-update) | async-done | bytes 1048592 | tf_op jit(solution)/shard_map/reduce_scatter | solution.py:63
  255.0 79.6 %reduce-scatter.6.cloned.1.call-done = f32[64,32,128]{2,0,1:T(8,128)} async-done(((f32[256,32,128]{2,0,1:T(8,128)}), f32[64,32,128]{2,0,1:T(8,128)}) %reduce-scatter.6.cloned.1.call-update) | async-done | bytes 1048592 | tf_op jit(solution)/shard_map/reduce_scatter | solution.py:62
  334.6 79.5 %reduce-scatter.8.cloned.1.call-done = f32[64,32,128]{2,0,1:T(8,128)} async-done(((f32[256,32,128]{2,0,1:T(8,128)}), f32[64,32,128]{2,0,1:T(8,128)}) %reduce-scatter.8.cloned.1.call-update) | async-done | bytes 1048592 | tf_op jit(solution)/shard_map/reduce_scatter | solution.py:64
  414.1 2.6 fusion.23
  416.7 1.6 copy.34
  418.4 3.6 all-to-all-start.2
  423.5 1.7 copy.33
  425.1 12.3 %all-to-all-done.2 = f32[64,8,4,128]{3,2,0,1:T(4,128)S(1)} async-done(((f32[64,8,4,128]{3,2,0,1:T(4,128)}), f32[64,8,4,128]{3,2,0,1:T(4,128)S(1)}, u32[]{:S(2)}, u32[]{:S(2)}) %all-to-all-start.2) | async-done | bytes 1048608 | tf_op jit(solution)/shard_map/all_to_all | solution.py:73
  437.4 3.6 all-to-all-start.1
  441.2 4.4 compare_select_fusion.1
  446.3 23.5 %fusion.8 = f32[2048,512]{1,0:T(8,128)} fusion(s32[512]{0:T(512)S(1)} %fusion.24, s32[2048]{0:T(1024)S(1)} %iota_add_fusion, f32[64,8,4,128]{3,2,1,0:T(4,128)S(1)} %bitcast.94, f32[512]{0:T(512)S(1)} %broadcast_bitcast_fusion), kind=kOutput, calls=%fused_computation.22 | convolution fusion | flops 6457393152 | bytes 5255168 | tf_op jit(solution)/shard_map/dot_general | solution.py:93
  469.8 25.5 %subtract_multiply_fusion = f32[2048,512]{1,0:T(8,128)} fusion(f32[2048,512]{1,0:T(8,128)} %fusion.8, s32[512]{0:T(512)S(1)} %fusion.24, s32[2048]{0:T(1024)S(1)} %iota_add_fusion, f32[64,8,4,128]{3,2,1,0:T(4,128)S(1)} %bitcast.95, f32[512]{0:T(512)S(1)} %broadcast_bitcast_fusion), kind=kOutput, calls=%fused_computation.21 | convolution fusion | flops 6459490304 | bytes 9449472 | tf_op jit(solution)/shard_map/dot_general | solution.py:87
  495.4 77.7 %reduce-scatter.14.cloned.1.call-done = f32[512,512]{1,0:T(8,128)} async-done(((f32[2048,512]{1,0:T(8,128)}), f32[512,512]{1,0:T(8,128)}) %reduce-scatter.14.cloned.1.call-update) | async-done | bytes 1048592 | tf_op jit(solution)/shard_map/reduce_scatter | solution.py:99
  573.0 2.5 reshape.186
  (35 shorter events, 5.6 us)
Async XLA Ops:
  6.5 11.0 %copy-start.1 = (s32[4,2]{0,1:T(2,128)S(1)}, s32[4,2]{0,1:T(2,128)}, u32[]{:S(2)}) copy-start(s32[4,2]{0,1:T(2,128)} %param.6) | copy-start | bytes 100
  12.3 55.0 %all-to-all-start = ((bf16[1,2,2048,256]{3,1,0,2:T(2,128)(2,1)}), bf16[1,2,2048,256]{3,1,0,2:T(2,128)(2,1)S(1)}, u32[]{:S(2)}, u32[]{:S(2)}) async-start(bf16[1,2,2048,256]{3,1,0,2:T(2,128)(2,1)} %copy.23), calls=%async_computation | async-start | bytes 4194304 | tf_op jit(solution)/shard_map/all_to_all | solution.py:59
  17.5 157.7 %reduce-scatter.10.cloned.1.call-start = ((), (), s32[]{:S(2)}) async-start(), calls=%async_computation.10 | async-start | bytes 5242880 | tf_op jit(solution)/shard_map/reduce_scatter | solution.py:65
  17.6 26.2 %collective-permute-start = (s32[4,2]{0,1:T(2,128)S(1)}, s32[4,2]{0,1:T(2,128)S(1)}, u32[]{:S(2)}, u32[]{:S(2)}) collective-permute-start(s32[4,2]{0,1:T(2,128)S(1)} %copy-done.1), channel_id=1, source_target_pairs={{0,1},{1,2},{2,3},{3,4},{4,5},{5,6},{6,7},{7,0},{8,9},{9,10},{10,1... | collective-permute-start | bytes 104 | tf_op jit(solution)/shard_map/ppermute | solution.py:52
  43.7 3.9 collective-permute-start.1
  47.6 3.9 collective-permute-start.2
  51.5 3.9 collective-permute-start.3
  55.4 3.9 collective-permute-start.4
  59.3 3.9 collective-permute-start.5
  63.2 3.9 collective-permute-start.6
  82.1 3.4 copy-start
  99.0 156.0 %reduce-scatter.12.cloned.1.call-start = ((), (), s32[]{:S(2)}) async-start(), calls=%async_computation.11 | async-start | bytes 5242880 | tf_op jit(solution)/shard_map/reduce_scatter | solution.py:63
  99.7 234.8 %reduce-scatter.6.cloned.1.call-start = ((), (), s32[]{:S(2)}) async-start(), calls=%async_computation.8 | async-start | bytes 5242880 | tf_op jit(solution)/shard_map/reduce_scatter | solution.py:62
  100.5 313.7 %reduce-scatter.8.cloned.1.call-start = ((), (), s32[]{:S(2)}) async-start(), calls=%async_computation.9 | async-start | bytes 5242880 | tf_op jit(solution)/shard_map/reduce_scatter | solution.py:64
  418.4 19.1 %all-to-all-start.2 = ((f32[64,8,4,128]{3,2,0,1:T(4,128)}), f32[64,8,4,128]{3,2,0,1:T(4,128)S(1)}, u32[]{:S(2)}, u32[]{:S(2)}) async-start(f32[64,8,4,128]{3,2,0,1:T(4,128)} %copy.34), calls=%async_computation.6 | async-start | bytes 2097152 | tf_op jit(solution)/shard_map/all_to_all | solution.py:73
  437.4 32.4 %all-to-all-start.1 = ((f32[64,8,4,128]{3,2,0,1:T(4,128)}), f32[64,8,4,128]{3,2,0,1:T(4,128)S(1)}, u32[]{:S(2)}, u32[]{:S(2)}) async-start(f32[64,8,4,128]{3,2,0,1:T(4,128)} %copy.33), calls=%async_computation.4 | async-start | bytes 2097152 | tf_op jit(solution)/shard_map/all_to_all | solution.py:72
  441.0 132.0 %reduce-scatter.14.cloned.1.call-start = ((), (), s32[]{:S(2)}) async-start(), calls=%async_computation.12 | async-start | bytes 5242880 | tf_op jit(solution)/shard_map/reduce_scatter | solution.py:99
Sparse Core Ops, SparseCore 0:
  99.1 76.1 reduce-scatter.9
  177.6 77.2 reduce-scatter.11
  257.3 77.2 reduce-scatter.5
  336.8 77.2 reduce-scatter.7
  495.5 77.5 reduce-scatter.13
